TPU v7x, 32 devices: a whole 2x2x4 slice. The times are simulated.
32 devices in a mesh: stream: 8 (over z, x), cross: 4 (over y, core).
Axes of the slice: x: 2, y: 2, z: 4, core: 2. Of those that a mesh axis runs over, the one named last changes fastest.
Arguments:
- adjoint: float32 [5, 32, 4096], P(None, 'stream', 'cross'), may hold values from -6 to 6
- source: float32 [5, 32, 4096], P(None, 'stream', 'cross'), may hold values from -30 to 30
- shape_grad: float32 [5, 32, 4096], P(None, 'stream', 'cross'), may hold values from -6 to 6
- lower_band: float32 [2, 5, 32, 4096], P(None, None, 'stream', 'cross'), may hold values from -1.5 to 0.5
- upper_band: float32 [3, 5, 32, 4096], P(None, None, 'stream', 'cross'), may hold values from -6 to 2, as said below
- jacobian: float32 [5, 5], replicated, may hold values from -2.5 to 2.5
- left_vectors: float32 [5, 5], replicated, may hold values from -1 to 2
- right_vectors: float32 [5, 5], replicated, may hold values from -1 to 2
- ctrl_local: int32 [32, 4096], P('stream', 'cross'), may hold values from 0 to 65535
Outputs:
- adjoint_next: float32 [5, 32, 4096], P(None, 'stream', 'cross')
- sensitivity: float32 [524288], P(('stream', 'cross'))
Inputs may be any that keep to these rules, and one draw needn't show every extreme that they name: upper_band[0] lies in 0.5 to 2.
All inputs are finite; a program needn't handle non-finite values.
Results may differ from a plain program's by a relative error of at most 0.00029.
Values sent between devices are 32-bit elements; how exact they have to be, the bound alone decides.
No kernel may reach another device: no remote copies, remote signals or barrier semaphores. Data moves between devices by JAX's collectives and lax.ppermute only.
A program may use at most 64 MiB of HBM per device.

v0:
```python
import functools

import jax
import jax.numpy as jnp
from jax import lax
from jax.experimental import pallas as pl
from jax.experimental.pallas import tpu as pltpu
from jax.sharding import PartitionSpec as P


NCTRL = 524288
LANES = 128
SUBLANES = 8

dissipation = 0.25
step_scale = 0.5
epsilon = 1e-06


VMEM = pl.BlockSpec(memory_space=pltpu.VMEM)
SMEM = pl.BlockSpec(memory_space=pltpu.SMEM)


def held(array):
    return pltpu.with_memory_space_constraint(array, pltpu.VMEM)


def round_up(value, step):
    return -(-value // step) * step


def mix(entry, columns):
    count = len(columns)
    return [
        sum(entry(f, g) * columns[g] for g in range(1, count)) + entry(f, 0) * columns[0]
        for f in range(count)
    ]


def scalars(matrix):
    return lambda f, g: matrix[f, g]


def table_rows(fields):
    return round_up(3 * fields * fields, SUBLANES)


def table_entries(table, fields, which):
    def entry(f, g):
        row = (which * fields + f) * fields + g
        return table[row : row + 1, :]

    return entry


CELL_KINDS = 5


def block_rows(fields, cells):
    return round_up(fields * (CELL_KINDS * cells + cells - 1 + 2), SUBLANES)


def spread(scratch, me, outs):
    for k, out in enumerate(outs):
        out[...] = scratch[lax.bitwise_xor(me[0], k)]


def pack_kernel(group, width, me, jac, left, right, adj, src, low, up, *refs):
    outs, (table, blocks, pad) = refs[:group], refs[group:]
    fields, cells, length = adj.shape
    for which, matrix in enumerate((jac, left, right)):
        for f in range(fields):
            for g in range(fields):
                row = (which * fields + f) * fields + g
                table[row : row + 1, :] = jnp.full((1, LANES), matrix[f, g], jnp.float32)
    rows = block_rows(fields, cells)
    if width < LANES or rows > fields * (CELL_KINDS * cells + cells + 1):
        blocks[...] = jnp.zeros_like(blocks)
    pad[...] = jnp.zeros_like(pad)
    for f in range(fields):
        pad[f, 1 : cells + 1, :] = adj[f]
    ahead = [pad[f, 2 : cells + 2, :] for f in range(fields)]
    behind = [pad[f, 0:cells, :] for f in range(fields)]
    central = mix(scalars(jac), [a - b for a, b in zip(ahead, behind)])
    residual = [
        src[f] - 0.5 * central[f] + dissipation * (ahead[f] - 2.0 * adj[f] + behind[f])
        for f in range(fields)
    ]
    characteristic = mix(scalars(left), residual)
    cell = lax.broadcasted_iota(jnp.int32, (cells, length), 0)
    extra = CELL_KINDS * fields * cells
    for f in range(fields):
        diagonal = up[0, f]
        inverse = 1.0 / diagonal
        own = jnp.where(cell == 1, inverse, 1.0)
        diagonal_1 = jnp.broadcast_to(up[0, f, 1:2, :], (cells, length))
        values = (
            characteristic[f] * own,
            low[0, f] * jnp.where(cell == 2, diagonal_1, own),
            low[1, f] * jnp.where(cell == 3, diagonal_1, own),
            up[1, f] * inverse,
            up[2, f] * inverse,
        )
        for d, base, lanes, to in pieces(group, width, rows):
            for k, value in enumerate(values):
                at = base + (k * fields + f) * cells
                blocks[d, at : at + cells, to] = value[:, lanes]
            at = base + extra + f * (cells + 1)
            blocks[d, at : at + 1, to] = inverse[0:1, lanes]
            blocks[d, at + 1 : at + cells - 1, to] = inverse[2:cells, lanes]
            blocks[d, at + cells - 1 : at + cells, to] = adj[f, 0:1, lanes]
            blocks[d, at + cells : at + cells + 1, to] = adj[f, cells - 1 : cells, lanes]
    spread(blocks, me, outs)


def pieces(group, width, rows):
    step = min(width, LANES)
    for d in range(group):
        for b in range(width // step):
            start = d * width + b * step
            yield d, b * rows, slice(start, start + step), slice(0, step)


class Lines:
    def __init__(self, ref, fields, cells, base):
        self.ref, self.fields, self.cells, self.base = ref, fields, cells, base

    def value(self, d, k, i):
        at = self.base(d) + k * self.fields * self.cells + i
        return self.ref[pl.ds(at, self.fields, stride=self.cells), :]

    def divided(self, d, i, value):
        if i == 1:
            return value
        at = self.base(d) + CELL_KINDS * self.fields * self.cells + (i if i == 0 else i - 1)
        return value * self.ref[pl.ds(at, self.fields, stride=self.cells + 1), :]


def less(value, factor, other):
    if other is None:
        return value
    return -(factor * other) if value is None else value - factor * other


SLOTS = 8


def sweep_kernel(group, fields, cells, me, half, table, *refs):
    jac, left = table_entries(table, fields, 0), table_entries(table, fields, 1)
    received, (lines, edge, message) = refs[:group], refs[group:]
    rows = block_rows(fields, cells)
    size = received[0].shape[0]
    count = size // rows
    for k in range(group):
        at = pl.multiple_of(lax.bitwise_xor(me[0], k) * size, SUBLANES)
        lines[pl.ds(at, size), :] = received[k][...]
    lower_half = jnp.full((fields, LANES), half[0], jnp.int32) == 0
    extra = CELL_KINDS * fields * cells
    for b in range(count):

        def across(row):
            return lines[pl.ds(b * rows + row, group, stride=size), :]

        firsts = [across(extra + f * (cells + 1) + cells - 1) for f in range(fields)]
        lasts = [across(extra + f * (cells + 1) + cells) for f in range(fields)]
        from_last = mix(jac, lasts)
        from_first = mix(jac, firsts)
        into_first = mix(left, [0.5 * x + dissipation * y for x, y in zip(from_last, lasts)])
        into_last = mix(left, [dissipation * y - 0.5 * x for x, y in zip(from_first, firsts)])
        at = 2 * b * fields * group
        for f in range(fields):
            edge[at + f * group : at + (f + 1) * group, :] = into_first[f]
            edge[at + (fields + f) * group : at + (fields + f + 1) * group, :] = into_last[f]

        def to_next(d):
            return edge[pl.ds(at + d, fields, stride=group), :]

        def to_previous(d):
            return edge[pl.ds(at + fields * group + d, fields, stride=group), :]

        view = Lines(lines, fields, cells, lambda d: (d * count + b) * rows)
        ones = jnp.ones((fields, LANES), jnp.float32)
        one, two = [None, ones, None], [None, None, None]
        forward = {}
        for d in range(group):
            for i in range(cells):
                value = view.value(d, 0, i)
                if i == 0 and d > 0:
                    value = value + to_next(d - 1)
                if i == cells - 1 and d < group - 1:
                    value = value + to_previous(d + 1)
                start = [value, None, ones if d == 0 and i == 0 else None]
                first, second = view.value(d, 1, i), view.value(d, 2, i)
                now = [less(less(start[c], second, two[c]), first, one[c]) for c in range(3)]
                forward[d, i] = now
                one, two = now, one
        ends = [one[0], two[0], to_next(group - 1)]
        one, two = [None] * 3, [None] * 3
        for d in reversed(range(group)):
            for i in reversed(range(cells)):
                start = [view.divided(d, i, value) for value in forward[d, i]]
                first, second = view.value(d, 3, i), view.value(d, 4, i)
                now = [less(less(start[c], second, two[c]), first, one[c]) for c in range(3)]
                one, two = now, one
        begins = [one[0], two[0], to_previous(0)]
        slots = [jnp.where(lower_half, x, y) for x, y in zip(ends, begins)]
        slots += [one[1], two[1], one[2], two[2], view.value(0, 2, 0)]
        for k, value in enumerate(slots):
            row = (b * SLOTS + k) * fields
            message[row : row + fields, :] = value


def solve_kernel(group, fields, cells, me, half, table, lines, edge, mine, other, *refs):
    outs, (squares, whole, blocks) = refs[:group], refs[group:]
    rows = block_rows(fields, cells)
    size = lines.shape[0] // group
    count = size // rows
    total = group * cells
    lower_half = jnp.full((fields, LANES), half[0], jnp.int32) == 0
    summed = None
    for b in range(count):
        view = Lines(lines, fields, cells, lambda d: (d * count + b) * rows)
        at = 2 * b * fields * group

        def to_next(d):
            return edge[pl.ds(at + d, fields, stride=group), :]

        def to_previous(d):
            return edge[pl.ds(at + fields * group + d, fields, stride=group), :]

        def slot(ref, k):
            row = (b * SLOTS + k) * fields
            return ref[row : row + fields, :]

        def of_lower(k):
            return jnp.where(lower_half, slot(mine, k), slot(other, k))

        def of_upper(k):
            return jnp.where(lower_half, slot(other, k), slot(mine, k))

        zeros = jnp.zeros((fields, LANES), jnp.float32)
        onto_last, onto_first = of_upper(2), of_lower(2)
        before, before_2 = of_lower(0) + onto_last, of_lower(1)
        added = onto_first - of_upper(7) * before_2
        after = of_upper(0) + of_upper(3) * before + of_upper(5) * added
        after_2 = of_upper(1) + of_upper(4) * before + of_upper(6) * added
        one, two = jnp.where(lower_half, zeros, before), jnp.where(lower_half, zeros, before_2)
        onto_first = jnp.where(lower_half, zeros, onto_first)
        onto_last = jnp.where(lower_half, onto_last, zeros)
        forward = {}
        for d in range(group):
            for i in range(cells):
                value = view.value(d, 0, i)
                if i == 0:
                    value = value + (to_next(d - 1) if d > 0 else onto_first)
                if i == cells - 1:
                    value = value + (to_previous(d + 1) if d < group - 1 else onto_last)
                value = less(less(value, view.value(d, 2, i), two), view.value(d, 1, i), one)
                forward[d, i] = value
                one, two = value, one
        one, two = jnp.where(lower_half, after, zeros), jnp.where(lower_half, after_2, zeros)
        for d in reversed(range(group)):
            for i in reversed(range(cells)):
                value = view.divided(d, i, forward[d, i])
                value = less(less(value, view.value(d, 4, i), two), view.value(d, 3, i), one)
                whole[pl.ds(b * fields * total + d * cells + i, fields, stride=total), :] = value
                one, two = value, one
        columns = [(b * fields + g) * total for g in range(fields)]
        increment = mix(table_entries(table, fields, 2), [whole[at : at + total, :] for at in columns])
        for f in range(fields):
            part = jnp.sum(increment[f] * increment[f], axis=0, keepdims=True)
            summed = part if summed is None else summed + part
            for d in range(group):
                row = (b * fields + f) * cells
                blocks[d, row : row + cells, :] = increment[f][d * cells : (d + 1) * cells, :]
    spread(blocks, me, outs)
    for n in range(squares.shape[0]):
        squares[n] = summed


def slab_kernel(peers, me, adj, grad, ctrl, *outs):
    fields, cells, length = adj.shape
    height = outs[0].shape[0]
    contribution = adj[0] * grad[0]
    for f in range(1, fields):
        contribution = contribution + adj[f] * grad[f]
    upper = contribution.astype(jnp.bfloat16).astype(jnp.float32)
    lower = contribution - upper
    high = lax.shift_right_logical(ctrl[...], 7)
    low = lax.bitwise_and(ctrl[...], LANES - 1)
    block = lax.broadcasted_iota(jnp.int32, (height, length), 0)
    lane = lax.broadcasted_iota(jnp.int32, (LANES, length), 0)
    sums = None
    for i in range(cells):
        hit = lane == low[i : i + 1, :]
        terms = jnp.concatenate(
            [
                jnp.where(hit, upper[i : i + 1, :], 0.0).astype(jnp.bfloat16),
                jnp.where(hit, lower[i : i + 1, :], 0.0).astype(jnp.bfloat16),
            ],
            axis=0,
        )
        rows = []
        for k in range(peers):
            offset = lax.bitwise_xor(me[0], k) * height
            rows.append(jnp.where(block == high[i : i + 1, :] - offset, 1.0, 0.0).astype(jnp.bfloat16))
        picked = jnp.concatenate(rows, axis=0)
        part = lax.dot_general(
            picked, terms, (((1,), (1,)), ((), ())), preferred_element_type=jnp.float32
        )
        sums = part if sums is None else sums + part
    sums = sums[:, :LANES] + sums[:, LANES:]
    for k in range(peers):
        outs[k][...] = sums[k * height : (k + 1) * height, :]


def finish_kernel(group, width, peers, cell_count, me, adj, squares, *refs):
    moved, slabs, (out, sens, blocks) = refs[:group], refs[group : group + peers], refs[group + peers :]
    fields, cells, _ = adj.shape
    for k in range(group):
        blocks[lax.bitwise_xor(me[0], k)] = moved[k][...]
    slab = slabs[0][...]
    for k in range(1, peers):
        slab = slab + slabs[k][...]
    sens[...] = slab
    total = jnp.sum(jnp.sum(squares[...], axis=0), axis=1, keepdims=True)
    factor = step_scale / jnp.sqrt(total / cell_count + epsilon)
    for d, base, lanes, to in pieces(group, width, fields * cells):
        for f in range(fields):
            at = base + f * cells
            out[f, :, lanes] = adj[f, :, lanes] + factor * blocks[d, at : at + cells, to]


def swap(array, axis, k):
    return lax.ppermute(array, axis, [(i, i ^ k) for i in range(lax.axis_size(axis))])


def exchange(arrays, axis):
    out = [arrays[0]]
    for k in range(1, len(arrays)):
        out.append(swap(arrays[k], axis, k))
    return out


def step(
    adjoint, source, shape_grad, lower_band, upper_band, jacobian, left_vectors, right_vectors, ctrl_local
):
    fields, cells, length = adjoint.shape
    parts, peers = lax.axis_size("stream"), lax.axis_size("cross")
    group = parts // 2
    width = length // group
    count = -(-width // LANES)
    rows = count * block_rows(fields, cells)
    back = count * fields * cells
    f32 = jnp.float32

    at = lax.axis_index("stream").astype(jnp.int32)
    me, half = lax.rem(at, group).reshape(1), lax.div(at, group).reshape(1)
    *packed, table = pl.pallas_call(
        functools.partial(pack_kernel, group, width),
        out_shape=[pltpu.VMEM((rows, LANES), f32)] * group
        + [pltpu.VMEM((table_rows(fields), LANES), f32)],
        in_specs=[SMEM] * 4 + [VMEM] * 4,
        out_specs=[VMEM] * (group + 1),
        scratch_shapes=[
            pltpu.VMEM((group, rows, LANES), f32),
            pltpu.VMEM((fields, round_up(cells + 2, SUBLANES), length), f32),
        ],
        name="pack",
    )(me, jacobian, left_vectors, right_vectors, adjoint, source, lower_band, upper_band)
    received = exchange(packed, "stream")

    height = NCTRL // (parts * peers * LANES)
    column = lax.axis_index("cross").astype(jnp.int32).reshape(1)
    slabs = pl.pallas_call(
        functools.partial(slab_kernel, peers),
        out_shape=[pltpu.VMEM((height, LANES), f32)] * peers,
        in_specs=[SMEM, VMEM, VMEM, VMEM],
        out_specs=[VMEM] * peers,
        cost_estimate=pl.CostEstimate(
            flops=4 * cells * length * NCTRL // parts, bytes_accessed=4 << 20, transcendentals=0
        ),
        name="slab",
    )(column, held(adjoint), shape_grad, ctrl_local)

    lines, edge, message = pl.pallas_call(
        functools.partial(sweep_kernel, group, fields, cells),
        out_shape=[
            pltpu.VMEM((group * rows, LANES), f32),
            pltpu.VMEM((2 * count * fields * group, LANES), f32),
            pltpu.VMEM((count * SLOTS * fields, LANES), f32),
        ],
        in_specs=[SMEM] * 2 + [VMEM] * (1 + group),
        out_specs=[VMEM] * 3,
        name="sweep",
    )(me, half, *(held(a) for a in (table, *received)))
    other = swap(message, "stream", group)
    slabs = exchange(slabs, "cross")

    *moved, squares = pl.pallas_call(
        functools.partial(solve_kernel, group, fields, cells),
        out_shape=[pltpu.VMEM((back, LANES), f32)] * group
        + [pltpu.VMEM((parts * peers, 1, LANES), f32)],
        in_specs=[SMEM] * 2 + [VMEM] * 5,
        out_specs=[VMEM] * (group + 1),
        scratch_shapes=[
            pltpu.VMEM((count * fields * group * cells, LANES), f32),
            pltpu.VMEM((group, back, LANES), f32),
        ],
        name="solve",
    )(me, half, *(held(a) for a in (table, lines, edge, message, other)))
    squares = lax.all_to_all(squares, ("stream", "cross"), split_axis=0, concat_axis=0, tiled=True)
    moved = exchange(moved, "stream")

    cell_count = fields * cells * length * parts * peers
    adjoint_next, sensitivity = pl.pallas_call(
        functools.partial(finish_kernel, group, width, peers, cell_count),
        out_shape=[
            jax.ShapeDtypeStruct(adjoint.shape, f32),
            jax.ShapeDtypeStruct((height, LANES), f32),
        ],
        in_specs=[SMEM] + [VMEM] * (2 + group + peers),
        out_specs=[VMEM, VMEM],
        scratch_shapes=[pltpu.VMEM((group, back, LANES), f32)],
        name="finish",
    )(me, *(held(a) for a in (adjoint, squares, *moved, *slabs)))
    return adjoint_next, sensitivity.reshape(height * LANES)


def solution(mesh):
    in_specs = (
        P(None, "stream", "cross"),
        P(None, "stream", "cross"),
        P(None, "stream", "cross"),
        P(None, None, "stream", "cross"),
        P(None, None, "stream", "cross"),
        P(),
        P(),
        P(),
        P("stream", "cross"),
    )
    out_specs = (P(None, "stream", "cross"), P(("stream", "cross")))
    return jax.shard_map(step, mesh=mesh, in_specs=in_specs, out_specs=out_specs, check_vma=False)
```

profile of v0, /device:TPU:0, one launch (start us, length us, event | category | flops | bytes accessed | tf_op | source)
XLA Modules:
  0.0 33.9 jit_solution(2768457723578595166)
XLA Ops:
  0.6 0.0 copy-start
  0.6 1.5 %pack.1 = (f32[256,128]{1,0:T(8,128)S(1)}, f32[256,128]{1,0:T(8,128)S(1)}, f32[256,128]{1,0:T(8,128)S(1)}, f32[256,128]{1,0:T(8,128)S(1)}, f32[80,128]{1,0:T(8,128)S(1)}) custom-call(s32[1]{0:T(128)} %bitcast.me, f32[5,5]{1,0:T(8,128)} %jac.1, f32[5,5]{1,0:T(8,128)} %left.1, f32[5,5]{1,0:T(8,128)} %right.1, f32[5,4,1024]{2,1,0:T(4,128)} %adj.5, ...), custom_call_target="tpu_custom_call" | custom-call | tf_op jit(solution)/shard_map/pack/pallas_call | solution.py:359
  2.2 3.0 %collective-permute-start = (f32[256,128]{1,0:T(8,128)S(1)}, f32[256,128]{1,0:T(8,128)S(1)}, u32[]{:S(2)}, u32[]{:S(2)}) collective-permute-start(f32[256,128]{1,0:T(8,128)S(1)} %get-tuple-element.23), channel_id=1, source_target_pairs={{0,4},{4,0},{8,12},{12,8},{16,20},{20,16},{24,28},{28,24},{1,5},{5... | collective-permute-start | bytes 393224 | tf_op jit(solution)/shard_map/ppermute | solution.py:335
  5.2 1.6 %collective-permute-start.1 = (f32[256,128]{1,0:T(8,128)S(1)}, f32[256,128]{1,0:T(8,128)S(1)}, u32[]{:S(2)}, u32[]{:S(2)}) collective-permute-start(f32[256,128]{1,0:T(8,128)S(1)} %get-tuple-element.24), channel_id=1, source_target_pairs={{0,8},{4,12},{8,0},{12,4},{16,24},{20,28},{24,16},{28,20},{1,9},{5... | collective-permute-start | bytes 393224 | tf_op jit(solution)/shard_map/ppermute | solution.py:335
  6.8 0.0 collective-permute-start.2
  6.8 0.0 copy-done
  6.8 2.4 %slab.1 = (f32[128,128]{1,0:T(8,128)S(1)}, f32[128,128]{1,0:T(8,128)S(1)}, f32[128,128]{1,0:T(8,128)S(1)}, f32[128,128]{1,0:T(8,128)S(1)}) custom-call(s32[1]{0:T(128)} %bitcast.2.me, f32[5,4,1024]{2,1,0:T(4,128)S(1)} %copy-done, f32[5,4,1024]{2,1,0:T(4,128)} %grad.1, s32[4,1024]{1,0:T(4,128)} %ctrl.1), custom_call_target="tpu_custom_call" | custom-call | flops 1073741824 | bytes 4194304 | tf_op jit(solution)/shard_map/slab/pallas_call | solution.py:375
  9.2 0.1 collective-permute-start.7
  9.3 0.0 collective-permute-done.refs_1_
  9.3 2.3 %collective-permute-done.1.refs_2_ = f32[256,128]{1,0:T(8,128)S(1)} collective-permute-done((f32[256,128]{1,0:T(8,128)S(1)}, f32[256,128]{1,0:T(8,128)S(1)}, u32[]{:S(2)}, u32[]{:S(2)}) %collective-permute-start.1) | collective-permute-done | bytes 131104 | tf_op jit(solution)/shard_map/ppermute | solution.py:335
  11.6 1.2 %collective-permute-done.2.refs_3_ = f32[256,128]{1,0:T(8,128)S(1)} collective-permute-done((f32[256,128]{1,0:T(8,128)S(1)}, f32[256,128]{1,0:T(8,128)S(1)}, u32[]{:S(2)}, u32[]{:S(2)}) %collective-permute-start.2) | collective-permute-done | bytes 131104 | tf_op jit(solution)/shard_map/ppermute | solution.py:335
  12.8 0.2 sweep.1
  13.0 2.8 %collective-permute-start.3 = (f32[80,128]{1,0:T(8,128)S(1)}, f32[80,128]{1,0:T(8,128)S(1)}, u32[]{:S(2)}, u32[]{:S(2)}) collective-permute-start(f32[80,128]{1,0:T(8,128)S(1)} %get-tuple-element.28.mine), channel_id=1, source_target_pairs={{0,16},{4,20},{8,24},{12,28},{16,0},{20,4},{24,8},{28,12},{1,17},{... | collective-permute-start | bytes 122888 | tf_op jit(solution)/shard_map/ppermute | solution.py:335
  15.8 1.5 %collective-permute-start.8 = (f32[128,128]{1,0:T(8,128)S(1)}, f32[128,128]{1,0:T(8,128)S(1)}, u32[]{:S(2)}, u32[]{:S(2)}) collective-permute-start(f32[128,128]{1,0:T(8,128)S(1)} %get-tuple-element.36), channel_id=1, source_target_pairs={{0,2},{1,3},{2,0},{3,1},{4,6},{5,7},{6,4},{7,5},{8,10},{9,11},{10,... | collective-permute-start | bytes 196616 | tf_op jit(solution)/shard_map/ppermute | solution.py:335
  17.4 0.0 collective-permute-start.9
  17.4 0.6 %collective-permute-done.3.other = f32[80,128]{1,0:T(8,128)S(1)} collective-permute-done((f32[80,128]{1,0:T(8,128)S(1)}, f32[80,128]{1,0:T(8,128)S(1)}, u32[]{:S(2)}, u32[]{:S(2)}) %collective-permute-start.3) | collective-permute-done | bytes 40992 | tf_op jit(solution)/shard_map/ppermute | solution.py:335
  18.0 0.8 %solve.1 = (f32[40,128]{1,0:T(8,128)S(1)}, f32[40,128]{1,0:T(8,128)S(1)}, f32[40,128]{1,0:T(8,128)S(1)}, f32[40,128]{1,0:T(8,128)S(1)}, f32[32,1,128]{2,1,0:T(1,128)}) custom-call(s32[1]{0:T(128)} %bitcast.me, s32[1]{0:T(128)} %bitcast.1.half, f32[80,128]{1,0:T(8,128)S(1)} %get-tuple-element.21.table, f32[1024,128]{1,0:T(8,128)S(1)} %get-tuple-element.26.lines, ...), custom_call_target="tpu_custom_call" | custom-call | tf_op jit(solution)/shard_map/solve/pallas_call | solution.py:400
  18.7 6.3 %all-to-all-start = ((f32[32,1,128]{2,1,0:T(1,128)}), f32[32,1,128]{2,1,0:T(1,128)S(1)}, u32[]{:S(2)}, u32[]{:S(2)}) async-start(f32[32,1,128]{2,1,0:T(1,128)} %get-tuple-element.29), calls=%async_computation | async-start | bytes 32768 | tf_op jit(solution)/shard_map/all_to_all | solution.py:412
  25.1 1.8 %collective-permute-start.4 = (f32[40,128]{1,0:T(8,128)S(1)}, f32[40,128]{1,0:T(8,128)S(1)}, u32[]{:S(2)}, u32[]{:S(2)}) collective-permute-start(f32[40,128]{1,0:T(8,128)S(1)} %get-tuple-element.31), channel_id=1, source_target_pairs={{0,4},{4,0},{8,12},{12,8},{16,20},{20,16},{24,28},{28,24},{1,5},{5... | collective-permute-start | bytes 61448 | tf_op jit(solution)/shard_map/ppermute | solution.py:335
  26.9 1.5 %collective-permute-start.5 = (f32[40,128]{1,0:T(8,128)S(1)}, f32[40,128]{1,0:T(8,128)S(1)}, u32[]{:S(2)}, u32[]{:S(2)}) collective-permute-start(f32[40,128]{1,0:T(8,128)S(1)} %get-tuple-element.32), channel_id=1, source_target_pairs={{0,8},{4,12},{8,0},{12,4},{16,24},{20,28},{24,16},{28,20},{1,9},{5... | collective-permute-start | bytes 61448 | tf_op jit(solution)/shard_map/ppermute | solution.py:335
  28.4 0.0 collective-permute-done.7.refs_5_
  28.4 0.3 collective-permute-start.6
  28.7 0.0 collective-permute-done.8.refs_6_
  28.7 0.0 collective-permute-done.9.refs_7_
  28.7 0.3 collective-permute-done.4.refs_1_
  29.0 1.9 %collective-permute-done.5.refs_2_ = f32[40,128]{1,0:T(8,128)S(1)} collective-permute-done((f32[40,128]{1,0:T(8,128)S(1)}, f32[40,128]{1,0:T(8,128)S(1)}, u32[]{:S(2)}, u32[]{:S(2)}) %collective-permute-start.5) | collective-permute-done | bytes 20512 | tf_op jit(solution)/shard_map/ppermute | solution.py:335
  30.9 2.2 %collective-permute-done.6.refs_3_ = f32[40,128]{1,0:T(8,128)S(1)} collective-permute-done((f32[40,128]{1,0:T(8,128)S(1)}, f32[40,128]{1,0:T(8,128)S(1)}, u32[]{:S(2)}, u32[]{:S(2)}) %collective-permute-start.6) | collective-permute-done | bytes 20512 | tf_op jit(solution)/shard_map/ppermute | solution.py:335
  33.1 0.0 all-to-all-done.squares
  33.1 0.8 %finish.1 = (f32[5,4,1024]{2,1,0:T(4,128)}, f32[128,128]{1,0:T(8,128)}) custom-call(s32[1]{0:T(128)} %bitcast.me, f32[5,4,1024]{2,1,0:T(4,128)S(1)} %copy-done, f32[32,1,128]{2,1,0:T(1,128)S(1)} %all-to-all-done.squares, f32[40,128]{1,0:T(8,128)S(1)} %get-tuple-element.30.refs_0_, f32[40,128]{1,0:T(8,128)S(1)} %collective-permute-done.4.refs_1_, ...), custom_call_target="tpu_custom_call" | custom-call | tf_op jit(solution)/shard_map/finish/pallas_call | solution.py:416
Async XLA Ops:
  0.6 6.1 %copy-start = (f32[5,4,1024]{2,1,0:T(4,128)S(1)}, f32[5,4,1024]{2,1,0:T(4,128)}, u32[]{:S(2)}) copy-start(f32[5,4,1024]{2,1,0:T(4,128)} %adj.5) | copy-start | bytes 245764
  2.2 7.1 %collective-permute-start = (f32[256,128]{1,0:T(8,128)S(1)}, f32[256,128]{1,0:T(8,128)S(1)}, u32[]{:S(2)}, u32[]{:S(2)}) collective-permute-start(f32[256,128]{1,0:T(8,128)S(1)} %get-tuple-element.23), channel_id=1, source_target_pairs={{0,4},{4,0},{8,12},{12,8},{16,20},{20,16},{24,28},{28,24},{1,5},{5... | collective-permute-start | bytes 393224 | tf_op jit(solution)/shard_map/ppermute | solution.py:335
  5.2 6.4 %collective-permute-start.1 = (f32[256,128]{1,0:T(8,128)S(1)}, f32[256,128]{1,0:T(8,128)S(1)}, u32[]{:S(2)}, u32[]{:S(2)}) collective-permute-start(f32[256,128]{1,0:T(8,128)S(1)} %get-tuple-element.24), channel_id=1, source_target_pairs={{0,8},{4,12},{8,0},{12,4},{16,24},{20,28},{24,16},{28,20},{1,9},{5... | collective-permute-start | bytes 393224 | tf_op jit(solution)/shard_map/ppermute | solution.py:335
  6.8 6.0 %collective-permute-start.2 = (f32[256,128]{1,0:T(8,128)S(1)}, f32[256,128]{1,0:T(8,128)S(1)}, u32[]{:S(2)}, u32[]{:S(2)}) collective-permute-start(f32[256,128]{1,0:T(8,128)S(1)} %get-tuple-element.25), channel_id=1, source_target_pairs={{0,12},{4,8},{8,4},{12,0},{16,28},{20,24},{24,20},{28,16},{1,13},{... | collective-permute-start | bytes 393224 | tf_op jit(solution)/shard_map/ppermute | solution.py:335
  9.2 19.2 %collective-permute-start.7 = (f32[128,128]{1,0:T(8,128)S(1)}, f32[128,128]{1,0:T(8,128)S(1)}, u32[]{:S(2)}, u32[]{:S(2)}) collective-permute-start(f32[128,128]{1,0:T(8,128)S(1)} %get-tuple-element.35), channel_id=1, source_target_pairs={{0,1},{1,0},{2,3},{3,2},{4,5},{5,4},{6,7},{7,6},{8,9},{9,8},{10,11... | collective-permute-start | bytes 196616 | tf_op jit(solution)/shard_map/ppermute | solution.py:335
  13.0 5.0 %collective-permute-start.3 = (f32[80,128]{1,0:T(8,128)S(1)}, f32[80,128]{1,0:T(8,128)S(1)}, u32[]{:S(2)}, u32[]{:S(2)}) collective-permute-start(f32[80,128]{1,0:T(8,128)S(1)} %get-tuple-element.28.mine), channel_id=1, source_target_pairs={{0,16},{4,20},{8,24},{12,28},{16,0},{20,4},{24,8},{28,12},{1,17},{... | collective-permute-start | bytes 122888 | tf_op jit(solution)/shard_map/ppermute | solution.py:335
  15.8 12.8 %collective-permute-start.8 = (f32[128,128]{1,0:T(8,128)S(1)}, f32[128,128]{1,0:T(8,128)S(1)}, u32[]{:S(2)}, u32[]{:S(2)}) collective-permute-start(f32[128,128]{1,0:T(8,128)S(1)} %get-tuple-element.36), channel_id=1, source_target_pairs={{0,2},{1,3},{2,0},{3,1},{4,6},{5,7},{6,4},{7,5},{8,10},{9,11},{10,... | collective-permute-start | bytes 196616 | tf_op jit(solution)/shard_map/ppermute | solution.py:335
  17.4 11.3 %collective-permute-start.9 = (f32[128,128]{1,0:T(8,128)S(1)}, f32[128,128]{1,0:T(8,128)S(1)}, u32[]{:S(2)}, u32[]{:S(2)}) collective-permute-start(f32[128,128]{1,0:T(8,128)S(1)} %get-tuple-element.37), channel_id=1, source_target_pairs={{0,3},{1,2},{2,1},{3,0},{4,7},{5,6},{6,5},{7,4},{8,11},{9,10},{10,... | collective-permute-start | bytes 196616 | tf_op jit(solution)/shard_map/ppermute | solution.py:335
  18.7 14.3 %all-to-all-start = ((f32[32,1,128]{2,1,0:T(1,128)}), f32[32,1,128]{2,1,0:T(1,128)S(1)}, u32[]{:S(2)}, u32[]{:S(2)}) async-start(f32[32,1,128]{2,1,0:T(1,128)} %get-tuple-element.29), calls=%async_computation | async-start | bytes 32768 | tf_op jit(solution)/shard_map/all_to_all | solution.py:412
  25.1 3.9 %collective-permute-start.4 = (f32[40,128]{1,0:T(8,128)S(1)}, f32[40,128]{1,0:T(8,128)S(1)}, u32[]{:S(2)}, u32[]{:S(2)}) collective-permute-start(f32[40,128]{1,0:T(8,128)S(1)} %get-tuple-element.31), channel_id=1, source_target_pairs={{0,4},{4,0},{8,12},{12,8},{16,20},{20,16},{24,28},{28,24},{1,5},{5... | collective-permute-start | bytes 61448 | tf_op jit(solution)/shard_map/ppermute | solution.py:335
  26.9 3.9 %collective-permute-start.5 = (f32[40,128]{1,0:T(8,128)S(1)}, f32[40,128]{1,0:T(8,128)S(1)}, u32[]{:S(2)}, u32[]{:S(2)}) collective-permute-start(f32[40,128]{1,0:T(8,128)S(1)} %get-tuple-element.32), channel_id=1, source_target_pairs={{0,8},{4,12},{8,0},{12,4},{16,24},{20,28},{24,16},{28,20},{1,9},{5... | collective-permute-start | bytes 61448 | tf_op jit(solution)/shard_map/ppermute | solution.py:335
  28.4 4.7 %collective-permute-start.6 = (f32[40,128]{1,0:T(8,128)S(1)}, f32[40,128]{1,0:T(8,128)S(1)}, u32[]{:S(2)}, u32[]{:S(2)}) collective-permute-start(f32[40,128]{1,0:T(8,128)S(1)} %get-tuple-element.33), channel_id=1, source_target_pairs={{0,12},{4,8},{8,4},{12,0},{16,28},{20,24},{24,20},{28,16},{1,13},{... | collective-permute-start | bytes 61448 | tf_op jit(solution)/shard_map/ppermute | solution.py:335
where the time goes:
time: 34.1 us; the launch traced here: 33.9 us
  starting transfers between devices  18.9 us (55%)
  waiting for transfers between devices  8.55 us (25%)
  Pallas kernels  5.71 us (17%)
  between operations  0.7 us (2%)
    ppermute x10, starting transfers between devices, swap(): lax.ppermute(array, axis, [(i, i ^ k) for i in range(lax.axis_size(axis))])  12.6 us
    ppermute x10, waiting for transfers between devices, swap(): lax.ppermute(array, axis, [(i, i ^ k) for i in range(lax.axis_size(axis))])  8.54 us
    all_to_all x1, starting transfers between devices, step(): lax.all_to_all(squares, ('stream', 'cross'), split_axis=0, concat_axis=0,...  6.34 us
    pallas_call x1, Pallas kernels, step(): pl.pallas_call(functools.partial(slab_kernel, peers), out_shape=[pltpu.VM...  2.39 us
    pallas_call x1, Pallas kernels, step(): pl.pallas_call(functools.partial(pack_kernel, group, width), out_shape=[p...  1.51 us
    pallas_call x1, Pallas kernels, step(): pl.pallas_call(functools.partial(finish_kernel, group, width, peers, cell...  0.8 us
    pallas_call x1, Pallas kernels, step(): pl.pallas_call(functools.partial(solve_kernel, group, fields, cells), out...  0.78 us
  transfers between devices with their start and end apart: 11, of which 6 were waited for; matrix products, arithmetic and copies ran while one was open for 0% of the time, Pallas kernels for 10%

commit v1 on v0

--- a/solution.py
+++ b/solution.py
@@ -19,6 +19,7 @@
 
 VMEM = pl.BlockSpec(memory_space=pltpu.VMEM)
 SMEM = pl.BlockSpec(memory_space=pltpu.SMEM)
+ANY = pl.BlockSpec(memory_space=pl.ANY)
 
 
 def held(array):
@@ -65,20 +66,36 @@
         out[...] = scratch[lax.bitwise_xor(me[0], k)]
 
 
-def pack_kernel(group, width, me, jac, left, right, adj, src, low, up, *refs):
-    outs, (table, blocks, pad) = refs[:group], refs[group:]
+def pack_kernel(group, width, me, *refs):
+    sources, outs = refs[:7], refs[7 : 7 + group]
+    table, blocks, pad, jac, left, right, adj, src, low, up, arrived = refs[7 + group :]
+    copies = [
+        pltpu.make_async_copy(source, target, arrived.at[n])
+        for n, (source, target) in enumerate(zip(sources, (jac, left, right, adj, src, low, up)))
+    ]
+    for n in (3, 4, 0, 1, 2, 6, 5):
+        copies[n].start()
     fields, cells, length = adj.shape
+    rows = block_rows(fields, cells)
+    if width < LANES or rows > fields * (CELL_KINDS * cells + cells + 1):
+        blocks[...] = jnp.zeros_like(blocks)
+    pad[...] = jnp.zeros_like(pad)
+    cell = lax.broadcasted_iota(jnp.int32, (cells, length), 0)
+    extra = CELL_KINDS * fields * cells
+    copies[3].wait()
+    for f in range(fields):
+        pad[f, 1 : cells + 1, :] = adj[f]
+        for d, base, lanes, to in pieces(group, width, rows):
+            at = base + extra + f * (cells + 1) + cells - 1
+            blocks[d, at : at + 1, to] = adj[f, 0:1, lanes]
+            blocks[d, at + 1 : at + 2, to] = adj[f, cells - 1 : cells, lanes]
+    for n in (4, 0, 1, 2):
+        copies[n].wait()
     for which, matrix in enumerate((jac, left, right)):
         for f in range(fields):
             for g in range(fields):
                 row = (which * fields + f) * fields + g
                 table[row : row + 1, :] = jnp.full((1, LANES), matrix[f, g], jnp.float32)
-    rows = block_rows(fields, cells)
-    if width < LANES or rows > fields * (CELL_KINDS * cells + cells + 1):
-        blocks[...] = jnp.zeros_like(blocks)
-    pad[...] = jnp.zeros_like(pad)
-    for f in range(fields):
-        pad[f, 1 : cells + 1, :] = adj[f]
     ahead = [pad[f, 2 : cells + 2, :] for f in range(fields)]
     behind = [pad[f, 0:cells, :] for f in range(fields)]
     central = mix(scalars(jac), [a - b for a, b in zip(ahead, behind)])
@@ -87,8 +104,8 @@
         for f in range(fields)
     ]
     characteristic = mix(scalars(left), residual)
-    cell = lax.broadcasted_iota(jnp.int32, (cells, length), 0)
-    extra = CELL_KINDS * fields * cells
+    copies[6].wait()
+    copies[5].wait()
     for f in range(fields):
         diagonal = up[0, f]
         inverse = 1.0 / diagonal
@@ -108,8 +125,6 @@
             at = base + extra + f * (cells + 1)
             blocks[d, at : at + 1, to] = inverse[0:1, lanes]
             blocks[d, at + 1 : at + cells - 1, to] = inverse[2:cells, lanes]
-            blocks[d, at + cells - 1 : at + cells, to] = adj[f, 0:1, lanes]
-            blocks[d, at + cells : at + cells + 1, to] = adj[f, cells - 1 : cells, lanes]
     spread(blocks, me, outs)
 
 
@@ -278,9 +293,9 @@
         squares[n] = summed
 
 
-def slab_kernel(peers, me, adj, grad, ctrl, *outs):
+def slab_kernel(peers, me, adj, grad, ctrl, keep, send):
     fields, cells, length = adj.shape
-    height = outs[0].shape[0]
+    height = keep.shape[0] * 2 // peers
     contribution = adj[0] * grad[0]
     for f in range(1, fields):
         contribution = contribution + adj[f] * grad[f]
@@ -311,18 +326,23 @@
         sums = part if sums is None else sums + part
     sums = sums[:, :LANES] + sums[:, LANES:]
     for k in range(peers):
-        outs[k][...] = sums[k * height : (k + 1) * height, :]
-
-
-def finish_kernel(group, width, peers, cell_count, me, adj, squares, *refs):
-    moved, slabs, (out, sens, blocks) = refs[:group], refs[group : group + peers], refs[group + peers :]
+        out, at = (send if k % 2 else keep), k // 2 * height
+        out[at : at + height, :] = sums[k * height : (k + 1) * height, :]
+
+
+def halve_kernel(height, kept, received, keep, send):
+    for k in range(kept.shape[0] // height):
+        rows = slice(k * height, (k + 1) * height)
+        out, at = (send if k % 2 else keep), k // 2 * height
+        out[at : at + height, :] = kept[rows, :] + received[rows, :]
+
+
+def finish_kernel(group, width, cell_count, me, adj, squares, keep, gained, *refs):
+    moved, (out, sens, blocks) = refs[:group], refs[group:]
     fields, cells, _ = adj.shape
     for k in range(group):
         blocks[lax.bitwise_xor(me[0], k)] = moved[k][...]
-    slab = slabs[0][...]
-    for k in range(1, peers):
-        slab = slab + slabs[k][...]
-    sens[...] = slab
+    sens[...] = keep[...] + gained[...]
     total = jnp.sum(jnp.sum(squares[...], axis=0), axis=1, keepdims=True)
     factor = step_scale / jnp.sqrt(total / cell_count + epsilon)
     for d, base, lanes, to in pieces(group, width, fields * cells):
@@ -355,33 +375,53 @@
     f32 = jnp.float32
 
     at = lax.axis_index("stream").astype(jnp.int32)
-    me, half = lax.rem(at, group).reshape(1), lax.div(at, group).reshape(1)
+    me = lax.rem(at, group).reshape(1)
+    half = lax.div(at, group)
+    half = half.reshape(1)
     *packed, table = pl.pallas_call(
         functools.partial(pack_kernel, group, width),
         out_shape=[pltpu.VMEM((rows, LANES), f32)] * group
         + [pltpu.VMEM((table_rows(fields), LANES), f32)],
-        in_specs=[SMEM] * 4 + [VMEM] * 4,
+        in_specs=[SMEM] + [ANY] * 7,
         out_specs=[VMEM] * (group + 1),
         scratch_shapes=[
             pltpu.VMEM((group, rows, LANES), f32),
             pltpu.VMEM((fields, round_up(cells + 2, SUBLANES), length), f32),
-        ],
+        ]
+        + [pltpu.SMEM((fields, fields), f32)] * 3
+        + [
+            pltpu.VMEM(array.shape, f32) for array in (adjoint, source, lower_band, upper_band)
+        ]
+        + [pltpu.SemaphoreType.DMA((7,))],
         name="pack",
     )(me, jacobian, left_vectors, right_vectors, adjoint, source, lower_band, upper_band)
     received = exchange(packed, "stream")
 
     height = NCTRL // (parts * peers * LANES)
     column = lax.axis_index("cross").astype(jnp.int32).reshape(1)
-    slabs = pl.pallas_call(
+    keep, send = pl.pallas_call(
         functools.partial(slab_kernel, peers),
-        out_shape=[pltpu.VMEM((height, LANES), f32)] * peers,
+        out_shape=[pltpu.VMEM((peers // 2 * height, LANES), f32)] * 2,
         in_specs=[SMEM, VMEM, VMEM, VMEM],
-        out_specs=[VMEM] * peers,
+        out_specs=[VMEM] * 2,
         cost_estimate=pl.CostEstimate(
             flops=4 * cells * length * NCTRL // parts, bytes_accessed=4 << 20, transcendentals=0
         ),
         name="slab",
     )(column, held(adjoint), shape_grad, ctrl_local)
+
+    bit = 1
+    while True:
+        gained = swap(send, "cross", bit)
+        bit *= 2
+        if bit == peers:
+            break
+        keep, send = pl.pallas_call(
+            functools.partial(halve_kernel, height),
+            out_shape=[pltpu.VMEM((peers // bit // 2 * height, LANES), f32)] * 2,
+            in_specs=[VMEM] * 2,
+            out_specs=[VMEM] * 2,
+        )(held(keep), held(gained))
 
     lines, edge, message = pl.pallas_call(
         functools.partial(sweep_kernel, group, fields, cells),
@@ -395,7 +435,6 @@
         name="sweep",
     )(me, half, *(held(a) for a in (table, *received)))
     other = swap(message, "stream", group)
-    slabs = exchange(slabs, "cross")
 
     *moved, squares = pl.pallas_call(
         functools.partial(solve_kernel, group, fields, cells),
@@ -414,16 +453,16 @@
 
     cell_count = fields * cells * length * parts * peers
     adjoint_next, sensitivity = pl.pallas_call(
-        functools.partial(finish_kernel, group, width, peers, cell_count),
+        functools.partial(finish_kernel, group, width, cell_count),
         out_shape=[
             jax.ShapeDtypeStruct(adjoint.shape, f32),
             jax.ShapeDtypeStruct((height, LANES), f32),
         ],
-        in_specs=[SMEM] + [VMEM] * (2 + group + peers),
+        in_specs=[SMEM] + [VMEM] * (4 + group),
         out_specs=[VMEM, VMEM],
         scratch_shapes=[pltpu.VMEM((group, back, LANES), f32)],
         name="finish",
-    )(me, *(held(a) for a in (adjoint, squares, *moved, *slabs)))
+    )(me, *(held(a) for a in (adjoint, squares, keep, gained, *moved)))
     return adjoint_next, sensitivity.reshape(height * LANES)
 
 

time: 34.1 us -> 34 us (level)
    ppermute x10 -> x9, waiting for transfers between devices: 8.54 us -> 8.46 us  [swap(): lax.ppermute(array, axis, [(i, i ^ k) for i in range(lax.axis_size(axis))])]
    ppermute x10 -> x9, starting transfers between devices: 12.6 us -> 12.7 us  [swap(): lax.ppermute(array, axis, [(i, i ^ k) for i in range(lax.axis_size(axis))])]
    pallas_call x1 -> x2, Pallas kernels: 0.8 us -> 0.81 us  [the longest x1 0.79 us: step(): pl.pallas_call(functools.partial(finish_kernel, group, width, cell_count)...]
  transfers between devices with their start and end apart: 11 -> 10, of which waited for: 6 -> 6; matrix products, arithmetic and copies ran while one was open for 0% -> 0% of each run, Pallas kernels for 10% -> 10%
where the time goes in v1:
time: 34 us; the launch traced here: 33.8 us
  starting transfers between devices  19 us (56%)
  waiting for transfers between devices  8.47 us (25%)
  Pallas kernels  5.61 us (16%)
  between operations  0.7 us (2%)
    ppermute x9, starting transfers between devices, swap(): lax.ppermute(array, axis, [(i, i ^ k) for i in range(lax.axis_size(axis))])  12.7 us
    ppermute x9, waiting for transfers between devices, swap(): lax.ppermute(array, axis, [(i, i ^ k) for i in range(lax.axis_size(axis))])  8.46 us
    all_to_all x1, starting transfers between devices, step(): lax.all_to_all(squares, ('stream', 'cross'), split_axis=0, concat_axis=0,...  6.34 us
    pallas_call x1, Pallas kernels, step(): pl.pallas_call(functools.partial(slab_kernel, peers), out_shape=[pltpu.VM...  2.39 us
    pallas_call x1, Pallas kernels, step(): pl.pallas_call(functools.partial(pack_kernel, group, width), out_shape=[p...  1.4 us
    pallas_call x1, Pallas kernels, step(): pl.pallas_call(functools.partial(finish_kernel, group, width, cell_count)...  0.79 us
    pallas_call x1, Pallas kernels, step(): pl.pallas_call(functools.partial(solve_kernel, group, fields, cells), out...  0.77 us
  transfers between devices with their start and end apart: 10, of which 6 were waited for; matrix products, arithmetic and copies ran while one was open for 0% of the time, Pallas kernels for 10%

profile of v1, /device:TPU:0, one launch (start us, length us, event | category | flops | bytes accessed | tf_op | source)
XLA Modules:
  0.0 33.8 jit_solution(5778120389102621198)
XLA Ops:
  0.6 0.0 copy-start
  0.6 1.4 %pack.1 = (f32[256,128]{1,0:T(8,128)S(1)}, f32[256,128]{1,0:T(8,128)S(1)}, f32[256,128]{1,0:T(8,128)S(1)}, f32[256,128]{1,0:T(8,128)S(1)}, f32[80,128]{1,0:T(8,128)S(1)}) custom-call(s32[1]{0:T(128)} %bitcast.me, f32[5,5]{1,0:T(8,128)} %refs_0_.1, f32[5,5]{1,0:T(8,128)} %refs_1_.1, f32[5,5]{1,0:T(8,128)} %refs_2_.1, f32[5,4,1024]{2,1,0:T(4,128)} %adj.3, ...), custom_call_target="tpu_custom_call" | custom-call | tf_op jit(solution)/shard_map/pack/pallas_call | solution.py:381
  2.1 3.0 %collective-permute-start = (f32[256,128]{1,0:T(8,128)S(1)}, f32[256,128]{1,0:T(8,128)S(1)}, u32[]{:S(2)}, u32[]{:S(2)}) collective-permute-start(f32[256,128]{1,0:T(8,128)S(1)} %get-tuple-element.23), channel_id=1, source_target_pairs={{0,4},{4,0},{8,12},{12,8},{16,20},{20,16},{24,28},{28,24},{1,5},{5... | collective-permute-start | bytes 393224 | tf_op jit(solution)/shard_map/ppermute | solution.py:355
  5.1 1.6 %collective-permute-start.1 = (f32[256,128]{1,0:T(8,128)S(1)}, f32[256,128]{1,0:T(8,128)S(1)}, u32[]{:S(2)}, u32[]{:S(2)}) collective-permute-start(f32[256,128]{1,0:T(8,128)S(1)} %get-tuple-element.24), channel_id=1, source_target_pairs={{0,8},{4,12},{8,0},{12,4},{16,24},{20,28},{24,16},{28,20},{1,9},{5... | collective-permute-start | bytes 393224 | tf_op jit(solution)/shard_map/ppermute | solution.py:355
  6.7 0.0 collective-permute-start.2
  6.7 0.0 copy-done
  6.7 2.4 %slab.1 = (f32[256,128]{1,0:T(8,128)S(1)}, f32[256,128]{1,0:T(8,128)S(1)}) custom-call(s32[1]{0:T(128)} %bitcast.2.me, f32[5,4,1024]{2,1,0:T(4,128)S(1)} %copy-done, f32[5,4,1024]{2,1,0:T(4,128)} %grad.1, s32[4,1024]{1,0:T(4,128)} %ctrl.1), custom_call_target="tpu_custom_call" | custom-call | flops 1073741824 | bytes 4194304 | tf_op jit(solution)/shard_map/slab/pallas_call | solution.py:402
  9.1 0.1 collective-permute-start.4
  9.1 0.0 collective-permute-done.refs_1_
  9.2 2.3 %collective-permute-done.1.refs_2_ = f32[256,128]{1,0:T(8,128)S(1)} collective-permute-done((f32[256,128]{1,0:T(8,128)S(1)}, f32[256,128]{1,0:T(8,128)S(1)}, u32[]{:S(2)}, u32[]{:S(2)}) %collective-permute-start.1) | collective-permute-done | bytes 131104 | tf_op jit(solution)/shard_map/ppermute | solution.py:355
  11.5 1.2 %collective-permute-done.2.refs_3_ = f32[256,128]{1,0:T(8,128)S(1)} collective-permute-done((f32[256,128]{1,0:T(8,128)S(1)}, f32[256,128]{1,0:T(8,128)S(1)}, u32[]{:S(2)}, u32[]{:S(2)}) %collective-permute-start.2) | collective-permute-done | bytes 131104 | tf_op jit(solution)/shard_map/ppermute | solution.py:355
  12.7 0.2 sweep.1
  12.9 2.8 %collective-permute-start.3 = (f32[80,128]{1,0:T(8,128)S(1)}, f32[80,128]{1,0:T(8,128)S(1)}, u32[]{:S(2)}, u32[]{:S(2)}) collective-permute-start(f32[80,128]{1,0:T(8,128)S(1)} %get-tuple-element.28.mine), channel_id=1, source_target_pairs={{0,16},{4,20},{8,24},{12,28},{16,0},{20,4},{24,8},{28,12},{1,17},{... | collective-permute-start | bytes 122888 | tf_op jit(solution)/shard_map/ppermute | solution.py:355
  15.7 0.0 collective-permute-done.4.received
  15.8 1.6 %collective-permute-start.5 = (f32[128,128]{1,0:T(8,128)S(1)}, f32[128,128]{1,0:T(8,128)S(1)}, u32[]{:S(2)}, u32[]{:S(2)}) collective-permute-start(f32[128,128]{1,0:T(8,128)S(1)} %get-tuple-element.33), channel_id=1, source_target_pairs={{0,2},{1,3},{2,0},{3,1},{4,6},{5,7},{6,4},{7,5},{8,10},{9,11},{10,... | collective-permute-start | bytes 196616 | tf_op jit(solution)/shard_map/ppermute | solution.py:355
  17.3 0.5 %collective-permute-done.3.other = f32[80,128]{1,0:T(8,128)S(1)} collective-permute-done((f32[80,128]{1,0:T(8,128)S(1)}, f32[80,128]{1,0:T(8,128)S(1)}, u32[]{:S(2)}, u32[]{:S(2)}) %collective-permute-start.3) | collective-permute-done | bytes 40992 | tf_op jit(solution)/shard_map/ppermute | solution.py:355
  17.9 0.8 %solve.1 = (f32[40,128]{1,0:T(8,128)S(1)}, f32[40,128]{1,0:T(8,128)S(1)}, f32[40,128]{1,0:T(8,128)S(1)}, f32[40,128]{1,0:T(8,128)S(1)}, f32[32,1,128]{2,1,0:T(1,128)}) custom-call(s32[1]{0:T(128)} %bitcast.me, s32[1]{0:T(128)} %bitcast.1.half, f32[80,128]{1,0:T(8,128)S(1)} %get-tuple-element.21.table, f32[1024,128]{1,0:T(8,128)S(1)} %get-tuple-element.26.lines, ...), custom_call_target="tpu_custom_call" | custom-call | tf_op jit(solution)/shard_map/solve/pallas_call | solution.py:439
  18.6 6.3 %all-to-all-start = ((f32[32,1,128]{2,1,0:T(1,128)}), f32[32,1,128]{2,1,0:T(1,128)S(1)}, u32[]{:S(2)}, u32[]{:S(2)}) async-start(f32[32,1,128]{2,1,0:T(1,128)} %get-tuple-element.29), calls=%async_computation | async-start | bytes 32768 | tf_op jit(solution)/shard_map/all_to_all | solution.py:451
  25.0 1.8 %collective-permute-start.6 = (f32[40,128]{1,0:T(8,128)S(1)}, f32[40,128]{1,0:T(8,128)S(1)}, u32[]{:S(2)}, u32[]{:S(2)}) collective-permute-start(f32[40,128]{1,0:T(8,128)S(1)} %get-tuple-element.35), channel_id=1, source_target_pairs={{0,4},{4,0},{8,12},{12,8},{16,20},{20,16},{24,28},{28,24},{1,5},{5... | collective-permute-start | bytes 61448 | tf_op jit(solution)/shard_map/ppermute | solution.py:355
  26.8 1.5 %collective-permute-start.7 = (f32[40,128]{1,0:T(8,128)S(1)}, f32[40,128]{1,0:T(8,128)S(1)}, u32[]{:S(2)}, u32[]{:S(2)}) collective-permute-start(f32[40,128]{1,0:T(8,128)S(1)} %get-tuple-element.36), channel_id=1, source_target_pairs={{0,8},{4,12},{8,0},{12,4},{16,24},{20,28},{24,16},{28,20},{1,9},{5... | collective-permute-start | bytes 61448 | tf_op jit(solution)/shard_map/ppermute | solution.py:355
  28.3 0.3 collective-permute-start.8
  28.5 0.3 collective-permute-done.6.refs_1_
  28.9 1.9 %collective-permute-done.7.refs_2_ = f32[40,128]{1,0:T(8,128)S(1)} collective-permute-done((f32[40,128]{1,0:T(8,128)S(1)}, f32[40,128]{1,0:T(8,128)S(1)}, u32[]{:S(2)}, u32[]{:S(2)}) %collective-permute-start.7) | collective-permute-done | bytes 20512 | tf_op jit(solution)/shard_map/ppermute | solution.py:355
  30.8 2.2 %collective-permute-done.8.refs_3_ = f32[40,128]{1,0:T(8,128)S(1)} collective-permute-done((f32[40,128]{1,0:T(8,128)S(1)}, f32[40,128]{1,0:T(8,128)S(1)}, u32[]{:S(2)}, u32[]{:S(2)}) %collective-permute-start.8) | collective-permute-done | bytes 20512 | tf_op jit(solution)/shard_map/ppermute | solution.py:355
  33.0 0.0 collective-permute-done.5.gained
  33.0 0.0 all-to-all-done.squares
  33.0 0.8 %finish.1 = (f32[5,4,1024]{2,1,0:T(4,128)}, f32[128,128]{1,0:T(8,128)}) custom-call(s32[1]{0:T(128)} %bitcast.me, f32[5,4,1024]{2,1,0:T(4,128)S(1)} %copy-done, f32[32,1,128]{2,1,0:T(1,128)S(1)} %all-to-all-done.squares, f32[128,128]{1,0:T(8,128)S(1)} %get-tuple-element.32.keep, f32[128,128]{1,0:T(8,128)S(1)} %collective-permute-done.5.gained, ...), custom_call_target="tpu_custom_call" | custom-call | tf_op jit(solution)/shard_map/finish/pallas_call | solution.py:455
  (1 shorter events, 0.0 us)
Async XLA Ops:
  0.6 6.0 %copy-start = (f32[5,4,1024]{2,1,0:T(4,128)S(1)}, f32[5,4,1024]{2,1,0:T(4,128)}, u32[]{:S(2)}) copy-start(f32[5,4,1024]{2,1,0:T(4,128)} %adj.3) | copy-start | bytes 245764
  2.1 7.1 %collective-permute-start = (f32[256,128]{1,0:T(8,128)S(1)}, f32[256,128]{1,0:T(8,128)S(1)}, u32[]{:S(2)}, u32[]{:S(2)}) collective-permute-start(f32[256,128]{1,0:T(8,128)S(1)} %get-tuple-element.23), channel_id=1, source_target_pairs={{0,4},{4,0},{8,12},{12,8},{16,20},{20,16},{24,28},{28,24},{1,5},{5... | collective-permute-start | bytes 393224 | tf_op jit(solution)/shard_map/ppermute | solution.py:355
  5.1 6.4 %collective-permute-start.1 = (f32[256,128]{1,0:T(8,128)S(1)}, f32[256,128]{1,0:T(8,128)S(1)}, u32[]{:S(2)}, u32[]{:S(2)}) collective-permute-start(f32[256,128]{1,0:T(8,128)S(1)} %get-tuple-element.24), channel_id=1, source_target_pairs={{0,8},{4,12},{8,0},{12,4},{16,24},{20,28},{24,16},{28,20},{1,9},{5... | collective-permute-start | bytes 393224 | tf_op jit(solution)/shard_map/ppermute | solution.py:355
  6.7 6.0 %collective-permute-start.2 = (f32[256,128]{1,0:T(8,128)S(1)}, f32[256,128]{1,0:T(8,128)S(1)}, u32[]{:S(2)}, u32[]{:S(2)}) collective-permute-start(f32[256,128]{1,0:T(8,128)S(1)} %get-tuple-element.25), channel_id=1, source_target_pairs={{0,12},{4,8},{8,4},{12,0},{16,28},{20,24},{24,20},{28,16},{1,13},{... | collective-permute-start | bytes 393224 | tf_op jit(solution)/shard_map/ppermute | solution.py:355
  9.1 6.7 %collective-permute-start.4 = (f32[256,128]{1,0:T(8,128)S(1)}, f32[256,128]{1,0:T(8,128)S(1)}, u32[]{:S(2)}, u32[]{:S(2)}) collective-permute-start(f32[256,128]{1,0:T(8,128)S(1)} %get-tuple-element.31), channel_id=1, source_target_pairs={{0,1},{1,0},{2,3},{3,2},{4,5},{5,4},{6,7},{7,6},{8,9},{9,8},{10,11... | collective-permute-start | bytes 393224 | tf_op jit(solution)/shard_map/ppermute | solution.py:355
  12.9 5.0 %collective-permute-start.3 = (f32[80,128]{1,0:T(8,128)S(1)}, f32[80,128]{1,0:T(8,128)S(1)}, u32[]{:S(2)}, u32[]{:S(2)}) collective-permute-start(f32[80,128]{1,0:T(8,128)S(1)} %get-tuple-element.28.mine), channel_id=1, source_target_pairs={{0,16},{4,20},{8,24},{12,28},{16,0},{20,4},{24,8},{28,12},{1,17},{... | collective-permute-start | bytes 122888 | tf_op jit(solution)/shard_map/ppermute | solution.py:355
  15.8 17.2 %collective-permute-start.5 = (f32[128,128]{1,0:T(8,128)S(1)}, f32[128,128]{1,0:T(8,128)S(1)}, u32[]{:S(2)}, u32[]{:S(2)}) collective-permute-start(f32[128,128]{1,0:T(8,128)S(1)} %get-tuple-element.33), channel_id=1, source_target_pairs={{0,2},{1,3},{2,0},{3,1},{4,6},{5,7},{6,4},{7,5},{8,10},{9,11},{10,... | collective-permute-start | bytes 196616 | tf_op jit(solution)/shard_map/ppermute | solution.py:355
  18.6 14.3 %all-to-all-start = ((f32[32,1,128]{2,1,0:T(1,128)}), f32[32,1,128]{2,1,0:T(1,128)S(1)}, u32[]{:S(2)}, u32[]{:S(2)}) async-start(f32[32,1,128]{2,1,0:T(1,128)} %get-tuple-element.29), calls=%async_computation | async-start | bytes 32768 | tf_op jit(solution)/shard_map/all_to_all | solution.py:451
  25.0 3.9 %collective-permute-start.6 = (f32[40,128]{1,0:T(8,128)S(1)}, f32[40,128]{1,0:T(8,128)S(1)}, u32[]{:S(2)}, u32[]{:S(2)}) collective-permute-start(f32[40,128]{1,0:T(8,128)S(1)} %get-tuple-element.35), channel_id=1, source_target_pairs={{0,4},{4,0},{8,12},{12,8},{16,20},{20,16},{24,28},{28,24},{1,5},{5... | collective-permute-start | bytes 61448 | tf_op jit(solution)/shard_map/ppermute | solution.py:355
  26.8 3.9 %collective-permute-start.7 = (f32[40,128]{1,0:T(8,128)S(1)}, f32[40,128]{1,0:T(8,128)S(1)}, u32[]{:S(2)}, u32[]{:S(2)}) collective-permute-start(f32[40,128]{1,0:T(8,128)S(1)} %get-tuple-element.36), channel_id=1, source_target_pairs={{0,8},{4,12},{8,0},{12,4},{16,24},{20,28},{24,16},{28,20},{1,9},{5... | collective-permute-start | bytes 61448 | tf_op jit(solution)/shard_map/ppermute | solution.py:355
  28.3 4.7 %collective-permute-start.8 = (f32[40,128]{1,0:T(8,128)S(1)}, f32[40,128]{1,0:T(8,128)S(1)}, u32[]{:S(2)}, u32[]{:S(2)}) collective-permute-start(f32[40,128]{1,0:T(8,128)S(1)} %get-tuple-element.37), channel_id=1, source_target_pairs={{0,12},{4,8},{8,4},{12,0},{16,28},{20,24},{24,20},{28,16},{1,13},{... | collective-permute-start | bytes 61448 | tf_op jit(solution)/shard_map/ppermute | solution.py:355

commit v2 on v0

--- a/solution.py
+++ b/solution.py
@@ -409,7 +409,10 @@
         ],
         name="solve",
     )(me, half, *(held(a) for a in (table, lines, edge, message, other)))
-    squares = lax.all_to_all(squares, ("stream", "cross"), split_axis=0, concat_axis=0, tiled=True)
+    squares = lax.all_to_all(
+        squares, ("stream", "cross"), split_axis=0, concat_axis=0, tiled=True,
+        axis_index_groups=[list(range(parts * peers))[::-1]]
+    )
     moved = exchange(moved, "stream")
 
     cell_count = fields * cells * length * parts * peers

time: 34.1 us -> 34.1 us (level)
  no operation moved by 1% of the time
where the time goes in v2:
time: 34.1 us; the launch traced here: 33.9 us
  starting transfers between devices  18.9 us (55%)
  waiting for transfers between devices  8.55 us (25%)
  Pallas kernels  5.71 us (17%)
  between operations  0.7 us (2%)
    ppermute x10, starting transfers between devices, swap(): lax.ppermute(array, axis, [(i, i ^ k) for i in range(lax.axis_size(axis))])  12.6 us
    ppermute x10, waiting for transfers between devices, swap(): lax.ppermute(array, axis, [(i, i ^ k) for i in range(lax.axis_size(axis))])  8.54 us
    all_to_all x1, starting transfers between devices, step(): lax.all_to_all(squares, ('stream', 'cross'), split_axis=0, concat_axis=0,...  6.34 us
    pallas_call x1, Pallas kernels, step(): pl.pallas_call(functools.partial(slab_kernel, peers), out_shape=[pltpu.VM...  2.39 us
    pallas_call x1, Pallas kernels, step(): pl.pallas_call(functools.partial(pack_kernel, group, width), out_shape=[p...  1.51 us
    pallas_call x1, Pallas kernels, step(): pl.pallas_call(functools.partial(finish_kernel, group, width, peers, cell...  0.8 us
    pallas_call x1, Pallas kernels, step(): pl.pallas_call(functools.partial(solve_kernel, group, fields, cells), out...  0.78 us
  transfers between devices with their start and end apart: 11, of which 6 were waited for; matrix products, arithmetic and copies ran while one was open for 0% of the time, Pallas kernels for 10%

profile of v2, /device:TPU:0, one launch (start us, length us, event | category | flops | bytes accessed | tf_op | source)
XLA Modules:
  0.0 33.9 jit_solution(9216818180400798839)
XLA Ops:
  0.6 0.0 copy-start
  0.6 1.5 %pack.1 = (f32[256,128]{1,0:T(8,128)S(1)}, f32[256,128]{1,0:T(8,128)S(1)}, f32[256,128]{1,0:T(8,128)S(1)}, f32[256,128]{1,0:T(8,128)S(1)}, f32[80,128]{1,0:T(8,128)S(1)}) custom-call(s32[1]{0:T(128)} %bitcast.me, f32[5,5]{1,0:T(8,128)} %jac.1, f32[5,5]{1,0:T(8,128)} %left.1, f32[5,5]{1,0:T(8,128)} %right.1, f32[5,4,1024]{2,1,0:T(4,128)} %adj.5, ...), custom_call_target="tpu_custom_call" | custom-call | tf_op jit(solution)/shard_map/pack/pallas_call | solution.py:359
  2.2 3.0 %collective-permute-start = (f32[256,128]{1,0:T(8,128)S(1)}, f32[256,128]{1,0:T(8,128)S(1)}, u32[]{:S(2)}, u32[]{:S(2)}) collective-permute-start(f32[256,128]{1,0:T(8,128)S(1)} %get-tuple-element.23), channel_id=1, source_target_pairs={{0,4},{4,0},{8,12},{12,8},{16,20},{20,16},{24,28},{28,24},{1,5},{5... | collective-permute-start | bytes 393224 | tf_op jit(solution)/shard_map/ppermute | solution.py:335
  5.2 1.6 %collective-permute-start.1 = (f32[256,128]{1,0:T(8,128)S(1)}, f32[256,128]{1,0:T(8,128)S(1)}, u32[]{:S(2)}, u32[]{:S(2)}) collective-permute-start(f32[256,128]{1,0:T(8,128)S(1)} %get-tuple-element.24), channel_id=1, source_target_pairs={{0,8},{4,12},{8,0},{12,4},{16,24},{20,28},{24,16},{28,20},{1,9},{5... | collective-permute-start | bytes 393224 | tf_op jit(solution)/shard_map/ppermute | solution.py:335
  6.8 0.0 collective-permute-start.2
  6.8 0.0 copy-done
  6.8 2.4 %slab.1 = (f32[128,128]{1,0:T(8,128)S(1)}, f32[128,128]{1,0:T(8,128)S(1)}, f32[128,128]{1,0:T(8,128)S(1)}, f32[128,128]{1,0:T(8,128)S(1)}) custom-call(s32[1]{0:T(128)} %bitcast.2.me, f32[5,4,1024]{2,1,0:T(4,128)S(1)} %copy-done, f32[5,4,1024]{2,1,0:T(4,128)} %grad.1, s32[4,1024]{1,0:T(4,128)} %ctrl.1), custom_call_target="tpu_custom_call" | custom-call | flops 1073741824 | bytes 4194304 | tf_op jit(solution)/shard_map/slab/pallas_call | solution.py:375
  9.2 0.1 collective-permute-start.7
  9.3 0.0 collective-permute-done.refs_1_
  9.3 2.3 %collective-permute-done.1.refs_2_ = f32[256,128]{1,0:T(8,128)S(1)} collective-permute-done((f32[256,128]{1,0:T(8,128)S(1)}, f32[256,128]{1,0:T(8,128)S(1)}, u32[]{:S(2)}, u32[]{:S(2)}) %collective-permute-start.1) | collective-permute-done | bytes 131104 | tf_op jit(solution)/shard_map/ppermute | solution.py:335
  11.6 1.2 %collective-permute-done.2.refs_3_ = f32[256,128]{1,0:T(8,128)S(1)} collective-permute-done((f32[256,128]{1,0:T(8,128)S(1)}, f32[256,128]{1,0:T(8,128)S(1)}, u32[]{:S(2)}, u32[]{:S(2)}) %collective-permute-start.2) | collective-permute-done | bytes 131104 | tf_op jit(solution)/shard_map/ppermute | solution.py:335
  12.8 0.2 sweep.1
  13.0 2.8 %collective-permute-start.3 = (f32[80,128]{1,0:T(8,128)S(1)}, f32[80,128]{1,0:T(8,128)S(1)}, u32[]{:S(2)}, u32[]{:S(2)}) collective-permute-start(f32[80,128]{1,0:T(8,128)S(1)} %get-tuple-element.28.mine), channel_id=1, source_target_pairs={{0,16},{4,20},{8,24},{12,28},{16,0},{20,4},{24,8},{28,12},{1,17},{... | collective-permute-start | bytes 122888 | tf_op jit(solution)/shard_map/ppermute | solution.py:335
  15.8 1.5 %collective-permute-start.8 = (f32[128,128]{1,0:T(8,128)S(1)}, f32[128,128]{1,0:T(8,128)S(1)}, u32[]{:S(2)}, u32[]{:S(2)}) collective-permute-start(f32[128,128]{1,0:T(8,128)S(1)} %get-tuple-element.36), channel_id=1, source_target_pairs={{0,2},{1,3},{2,0},{3,1},{4,6},{5,7},{6,4},{7,5},{8,10},{9,11},{10,... | collective-permute-start | bytes 196616 | tf_op jit(solution)/shard_map/ppermute | solution.py:335
  17.4 0.0 collective-permute-start.9
  17.4 0.6 %collective-permute-done.3.other = f32[80,128]{1,0:T(8,128)S(1)} collective-permute-done((f32[80,128]{1,0:T(8,128)S(1)}, f32[80,128]{1,0:T(8,128)S(1)}, u32[]{:S(2)}, u32[]{:S(2)}) %collective-permute-start.3) | collective-permute-done | bytes 40992 | tf_op jit(solution)/shard_map/ppermute | solution.py:335
  18.0 0.8 %solve.1 = (f32[40,128]{1,0:T(8,128)S(1)}, f32[40,128]{1,0:T(8,128)S(1)}, f32[40,128]{1,0:T(8,128)S(1)}, f32[40,128]{1,0:T(8,128)S(1)}, f32[32,1,128]{2,1,0:T(1,128)}) custom-call(s32[1]{0:T(128)} %bitcast.me, s32[1]{0:T(128)} %bitcast.1.half, f32[80,128]{1,0:T(8,128)S(1)} %get-tuple-element.21.table, f32[1024,128]{1,0:T(8,128)S(1)} %get-tuple-element.26.lines, ...), custom_call_target="tpu_custom_call" | custom-call | tf_op jit(solution)/shard_map/solve/pallas_call | solution.py:400
  18.7 6.3 %all-to-all-start = ((f32[32,1,128]{2,1,0:T(1,128)}), f32[32,1,128]{2,1,0:T(1,128)S(1)}, u32[]{:S(2)}, u32[]{:S(2)}) async-start(f32[32,1,128]{2,1,0:T(1,128)} %get-tuple-element.29), calls=%async_computation | async-start | bytes 32768 | tf_op jit(solution)/shard_map/all_to_all | solution.py:412
  25.1 1.8 %collective-permute-start.4 = (f32[40,128]{1,0:T(8,128)S(1)}, f32[40,128]{1,0:T(8,128)S(1)}, u32[]{:S(2)}, u32[]{:S(2)}) collective-permute-start(f32[40,128]{1,0:T(8,128)S(1)} %get-tuple-element.31), channel_id=1, source_target_pairs={{0,4},{4,0},{8,12},{12,8},{16,20},{20,16},{24,28},{28,24},{1,5},{5... | collective-permute-start | bytes 61448 | tf_op jit(solution)/shard_map/ppermute | solution.py:335
  26.9 1.5 %collective-permute-start.5 = (f32[40,128]{1,0:T(8,128)S(1)}, f32[40,128]{1,0:T(8,128)S(1)}, u32[]{:S(2)}, u32[]{:S(2)}) collective-permute-start(f32[40,128]{1,0:T(8,128)S(1)} %get-tuple-element.32), channel_id=1, source_target_pairs={{0,8},{4,12},{8,0},{12,4},{16,24},{20,28},{24,16},{28,20},{1,9},{5... | collective-permute-start | bytes 61448 | tf_op jit(solution)/shard_map/ppermute | solution.py:335
  28.4 0.0 collective-permute-done.7.refs_5_
  28.4 0.3 collective-permute-start.6
  28.7 0.0 collective-permute-done.8.refs_6_
  28.7 0.0 collective-permute-done.9.refs_7_
  28.7 0.3 collective-permute-done.4.refs_1_
  29.0 1.9 %collective-permute-done.5.refs_2_ = f32[40,128]{1,0:T(8,128)S(1)} collective-permute-done((f32[40,128]{1,0:T(8,128)S(1)}, f32[40,128]{1,0:T(8,128)S(1)}, u32[]{:S(2)}, u32[]{:S(2)}) %collective-permute-start.5) | collective-permute-done | bytes 20512 | tf_op jit(solution)/shard_map/ppermute | solution.py:335
  30.9 2.2 %collective-permute-done.6.refs_3_ = f32[40,128]{1,0:T(8,128)S(1)} collective-permute-done((f32[40,128]{1,0:T(8,128)S(1)}, f32[40,128]{1,0:T(8,128)S(1)}, u32[]{:S(2)}, u32[]{:S(2)}) %collective-permute-start.6) | collective-permute-done | bytes 20512 | tf_op jit(solution)/shard_map/ppermute | solution.py:335
  33.1 0.0 all-to-all-done.squares
  33.1 0.8 %finish.1 = (f32[5,4,1024]{2,1,0:T(4,128)}, f32[128,128]{1,0:T(8,128)}) custom-call(s32[1]{0:T(128)} %bitcast.me, f32[5,4,1024]{2,1,0:T(4,128)S(1)} %copy-done, f32[32,1,128]{2,1,0:T(1,128)S(1)} %all-to-all-done.squares, f32[40,128]{1,0:T(8,128)S(1)} %get-tuple-element.30.refs_0_, f32[40,128]{1,0:T(8,128)S(1)} %collective-permute-done.4.refs_1_, ...), custom_call_target="tpu_custom_call" | custom-call | tf_op jit(solution)/shard_map/finish/pallas_call | solution.py:419
Async XLA Ops:
  0.6 6.1 %copy-start = (f32[5,4,1024]{2,1,0:T(4,128)S(1)}, f32[5,4,1024]{2,1,0:T(4,128)}, u32[]{:S(2)}) copy-start(f32[5,4,1024]{2,1,0:T(4,128)} %adj.5) | copy-start | bytes 245764
  2.2 7.1 %collective-permute-start = (f32[256,128]{1,0:T(8,128)S(1)}, f32[256,128]{1,0:T(8,128)S(1)}, u32[]{:S(2)}, u32[]{:S(2)}) collective-permute-start(f32[256,128]{1,0:T(8,128)S(1)} %get-tuple-element.23), channel_id=1, source_target_pairs={{0,4},{4,0},{8,12},{12,8},{16,20},{20,16},{24,28},{28,24},{1,5},{5... | collective-permute-start | bytes 393224 | tf_op jit(solution)/shard_map/ppermute | solution.py:335
  5.2 6.4 %collective-permute-start.1 = (f32[256,128]{1,0:T(8,128)S(1)}, f32[256,128]{1,0:T(8,128)S(1)}, u32[]{:S(2)}, u32[]{:S(2)}) collective-permute-start(f32[256,128]{1,0:T(8,128)S(1)} %get-tuple-element.24), channel_id=1, source_target_pairs={{0,8},{4,12},{8,0},{12,4},{16,24},{20,28},{24,16},{28,20},{1,9},{5... | collective-permute-start | bytes 393224 | tf_op jit(solution)/shard_map/ppermute | solution.py:335
  6.8 6.0 %collective-permute-start.2 = (f32[256,128]{1,0:T(8,128)S(1)}, f32[256,128]{1,0:T(8,128)S(1)}, u32[]{:S(2)}, u32[]{:S(2)}) collective-permute-start(f32[256,128]{1,0:T(8,128)S(1)} %get-tuple-element.25), channel_id=1, source_target_pairs={{0,12},{4,8},{8,4},{12,0},{16,28},{20,24},{24,20},{28,16},{1,13},{... | collective-permute-start | bytes 393224 | tf_op jit(solution)/shard_map/ppermute | solution.py:335
  9.2 19.2 %collective-permute-start.7 = (f32[128,128]{1,0:T(8,128)S(1)}, f32[128,128]{1,0:T(8,128)S(1)}, u32[]{:S(2)}, u32[]{:S(2)}) collective-permute-start(f32[128,128]{1,0:T(8,128)S(1)} %get-tuple-element.35), channel_id=1, source_target_pairs={{0,1},{1,0},{2,3},{3,2},{4,5},{5,4},{6,7},{7,6},{8,9},{9,8},{10,11... | collective-permute-start | bytes 196616 | tf_op jit(solution)/shard_map/ppermute | solution.py:335
  13.0 5.0 %collective-permute-start.3 = (f32[80,128]{1,0:T(8,128)S(1)}, f32[80,128]{1,0:T(8,128)S(1)}, u32[]{:S(2)}, u32[]{:S(2)}) collective-permute-start(f32[80,128]{1,0:T(8,128)S(1)} %get-tuple-element.28.mine), channel_id=1, source_target_pairs={{0,16},{4,20},{8,24},{12,28},{16,0},{20,4},{24,8},{28,12},{1,17},{... | collective-permute-start | bytes 122888 | tf_op jit(solution)/shard_map/ppermute | solution.py:335
  15.8 12.8 %collective-permute-start.8 = (f32[128,128]{1,0:T(8,128)S(1)}, f32[128,128]{1,0:T(8,128)S(1)}, u32[]{:S(2)}, u32[]{:S(2)}) collective-permute-start(f32[128,128]{1,0:T(8,128)S(1)} %get-tuple-element.36), channel_id=1, source_target_pairs={{0,2},{1,3},{2,0},{3,1},{4,6},{5,7},{6,4},{7,5},{8,10},{9,11},{10,... | collective-permute-start | bytes 196616 | tf_op jit(solution)/shard_map/ppermute | solution.py:335
  17.4 11.3 %collective-permute-start.9 = (f32[128,128]{1,0:T(8,128)S(1)}, f32[128,128]{1,0:T(8,128)S(1)}, u32[]{:S(2)}, u32[]{:S(2)}) collective-permute-start(f32[128,128]{1,0:T(8,128)S(1)} %get-tuple-element.37), channel_id=1, source_target_pairs={{0,3},{1,2},{2,1},{3,0},{4,7},{5,6},{6,5},{7,4},{8,11},{9,10},{10,... | collective-permute-start | bytes 196616 | tf_op jit(solution)/shard_map/ppermute | solution.py:335
  18.7 14.3 %all-to-all-start = ((f32[32,1,128]{2,1,0:T(1,128)}), f32[32,1,128]{2,1,0:T(1,128)S(1)}, u32[]{:S(2)}, u32[]{:S(2)}) async-start(f32[32,1,128]{2,1,0:T(1,128)} %get-tuple-element.29), calls=%async_computation | async-start | bytes 32768 | tf_op jit(solution)/shard_map/all_to_all | solution.py:412
  25.1 3.9 %collective-permute-start.4 = (f32[40,128]{1,0:T(8,128)S(1)}, f32[40,128]{1,0:T(8,128)S(1)}, u32[]{:S(2)}, u32[]{:S(2)}) collective-permute-start(f32[40,128]{1,0:T(8,128)S(1)} %get-tuple-element.31), channel_id=1, source_target_pairs={{0,4},{4,0},{8,12},{12,8},{16,20},{20,16},{24,28},{28,24},{1,5},{5... | collective-permute-start | bytes 61448 | tf_op jit(solution)/shard_map/ppermute | solution.py:335
  26.9 3.9 %collective-permute-start.5 = (f32[40,128]{1,0:T(8,128)S(1)}, f32[40,128]{1,0:T(8,128)S(1)}, u32[]{:S(2)}, u32[]{:S(2)}) collective-permute-start(f32[40,128]{1,0:T(8,128)S(1)} %get-tuple-element.32), channel_id=1, source_target_pairs={{0,8},{4,12},{8,0},{12,4},{16,24},{20,28},{24,16},{28,20},{1,9},{5... | collective-permute-start | bytes 61448 | tf_op jit(solution)/shard_map/ppermute | solution.py:335
  28.4 4.7 %collective-permute-start.6 = (f32[40,128]{1,0:T(8,128)S(1)}, f32[40,128]{1,0:T(8,128)S(1)}, u32[]{:S(2)}, u32[]{:S(2)}) collective-permute-start(f32[40,128]{1,0:T(8,128)S(1)} %get-tuple-element.33), channel_id=1, source_target_pairs={{0,12},{4,8},{8,4},{12,0},{16,28},{20,24},{24,20},{28,16},{1,13},{... | collective-permute-start | bytes 61448 | tf_op jit(solution)/shard_map/ppermute | solution.py:335
